TPU v7x, 256 devices: a whole 4x4x8 slice. The times are simulated.
256 devices in a mesh: gx: 8 (over y, core), gy: 4 (over z_lo), gz: 8 (over z_hi, x).
Axes of the slice: x: 4, y: 4, z: 8 (z_hi: 2, z_lo: 4; z = z_hi * 4 + z_lo), core: 2. Of those that a mesh axis runs over, the one named last changes fastest.
Arguments:
- tokens: bfloat16 [2048, 8192], P(('gx', 'gy'), 'gz'), may hold values from -6 to 6
- gate_weight: bfloat16 [8192, 28672], P('gz', ('gx', 'gy')), may hold values from -0.0625 to 0.0625
- up_weight: bfloat16 [8192, 28672], P('gz', ('gx', 'gy')), may hold values from -0.0625 to 0.0625
- down_weight: bfloat16 [28672, 8192], P(('gx', 'gy'), 'gz'), may hold values from -0.03125 to 0.03125
Outputs:
- layer_output: bfloat16 [2048, 8192], P(('gx', 'gy'), 'gz')
All inputs are finite; a program needn't handle non-finite values.
Results may differ from a plain program's by a relative error of at most 0.029.
Values may be sent and summed in bfloat16 or wider, within the bound.
A program may use at most 128 MiB of HBM per device.

v0:
```python
import jax
import jax.numpy as jnp
from jax import lax
from jax.sharding import PartitionSpec as P


def shards(tokens, gate_weight, up_weight, down_weight):
    gathered = lax.all_gather(tokens, "gx", axis=0, tiled=True)

    def column_product(weight_piece):
        return jnp.dot(gathered, weight_piece, preferred_element_type=jnp.float32)

    gate_partial = column_product(lax.all_gather(gate_weight, "gy", axis=1, tiled=True))
    up_partial = column_product(lax.all_gather(up_weight, "gy", axis=1, tiled=True))
    gate_sum, up_sum = (
        lax.psum_scatter(
            gate_partial.astype(jnp.bfloat16), "gz", scatter_dimension=0, tiled=True
        ).astype(jnp.float32),
        lax.psum_scatter(
            up_partial.astype(jnp.bfloat16), "gz", scatter_dimension=0, tiled=True
        ).astype(jnp.float32),
    )
    local_hidden = (jax.nn.silu(gate_sum) * up_sum).astype(jnp.bfloat16)
    hidden = lax.all_gather(local_hidden, "gz", axis=0, tiled=True)
    down_partial = jnp.dot(
        hidden,
        lax.all_gather(down_weight, "gy", axis=0, tiled=True),
        preferred_element_type=jnp.float32,
    )
    layer_output = lax.psum_scatter(
        down_partial.astype(jnp.bfloat16), "gx", scatter_dimension=0, tiled=True
    )
    return layer_output


def solution(mesh):
    return jax.shard_map(
        shards,
        mesh=mesh,
        in_specs=(
            P(("gx", "gy"), "gz"),
            P("gz", ("gx", "gy")),
            P("gz", ("gx", "gy")),
            P(("gx", "gy"), "gz"),
        ),
        out_specs=P(("gx", "gy"), "gz"),
        check_vma=False,
    )
```

profile of v0, /device:TPU:2, one launch (start us, length us, event | category | flops | bytes accessed | tf_op | source)
XLA Modules:
  0.0 839.3 jit_solution(120754620333667691)
XLA Ops:
  6.5 0.0 all-gather.6.cloned.1.call-start
  6.5 0.7 all-gather.6.cloned.1.call-update
  7.3 0.0 all-gather.8.cloned.1.call-start
  7.3 0.7 all-gather.8.cloned.1.call-update
  8.0 0.0 all-gather.10.cloned.1.call-start
  8.1 0.7 all-gather.10.cloned.1.call-update
  8.7 0.0 reduce-scatter.4.cloned.1.call-start
  8.8 29.3 %all-gather.6.cloned.1.call-done = bf16[512,1024]{1,0:T(8,128)(2,1)} async-done(((bf16[64,1024]{1,0:T(8,128)(2,1)}), bf16[512,1024]{1,0:T(8,128)(2,1)}) %all-gather.6.cloned.1.call-update) | async-done | bytes 1048592 | tf_op jit(solution)/shard_map/all_gather | solution.py:8
  38.1 0.0 copy-start
  38.1 137.6 %all-gather.8.cloned.1.call-done = bf16[1024,3584]{1,0:T(8,128)(2,1)} async-done(((bf16[1024,896]{1,0:T(8,128)(2,1)}), bf16[1024,3584]{1,0:T(8,128)(2,1)}) %all-gather.8.cloned.1.call-update) | async-done | bytes 7340048 | tf_op jit(solution)/shard_map/all_gather | solution.py:13
  175.7 9.2 %convolution_convert_fusion.1 = bf16[512,3584]{1,0:T(8,128)(2,1)} fusion(bf16[512,1024]{1,0:T(8,128)(2,1)} %all-gather.6.cloned.1.call-done, bf16[1024,3584]{1,0:T(8,128)(2,1)} %all-gather.8.cloned.1.call-done), kind=kOutput, calls=%fused_computation.1 | convolution fusion | flops 3759931392 | bytes 12058624 | tf_op jit(solution)/shard_map/dot_general | solution.py:11
  184.9 0.0 reduce-scatter.4.cloned.1.call-update
  184.9 0.0 reduce-scatter.6.cloned.1.call-start
  185.0 128.1 %all-gather.10.cloned.1.call-done = bf16[1024,3584]{1,0:T(8,128)(2,1)} async-done(((bf16[1024,896]{1,0:T(8,128)(2,1)}), bf16[1024,3584]{1,0:T(8,128)(2,1)}) %all-gather.10.cloned.1.call-update) | async-done | bytes 7340048 | tf_op jit(solution)/shard_map/all_gather | solution.py:14
  313.1 0.0 copy-done
  313.1 8.4 %convolution_convert_fusion = bf16[512,3584]{1,0:T(8,128)(2,1)} fusion(bf16[512,1024]{1,0:T(8,128)(2,1)S(1)} %copy-done, bf16[1024,3584]{1,0:T(8,128)(2,1)} %all-gather.10.cloned.1.call-done), kind=kOutput, calls=%fused_computation | convolution fusion | flops 3759931392 | bytes 12058624 | tf_op jit(solution)/shard_map/dot_general | solution.py:11
  321.5 0.0 reduce-scatter.6.cloned.1.call-update
  321.6 0.0 all-gather.14.cloned.1.call-start
  321.6 0.5 all-gather.14.cloned.1.call-update
  322.1 0.0 all-gather.12.cloned.1.call-start
  322.2 115.4 %reduce-scatter.4.cloned.1.call-done = bf16[64,3584]{1,0:T(8,128)(2,1)} async-done(((bf16[512,3584]{1,0:T(8,128)(2,1)}), bf16[64,3584]{1,0:T(8,128)(2,1)}) %reduce-scatter.4.cloned.1.call-update) | async-done | bytes 458768 | tf_op jit(solution)/shard_map/reduce_scatter | solution.py:16
  437.6 121.3 %reduce-scatter.6.cloned.1.call-done = bf16[64,3584]{1,0:T(8,128)(2,1)} async-done(((bf16[512,3584]{1,0:T(8,128)(2,1)}), bf16[64,3584]{1,0:T(8,128)(2,1)}) %reduce-scatter.6.cloned.1.call-update) | async-done | bytes 458768 | tf_op jit(solution)/shard_map/reduce_scatter | solution.py:19
  558.9 2.2 fusion.4
  561.1 0.0 all-gather.12.cloned.1.call-update
  561.1 0.0 reduce-scatter.8.cloned.1.call-start
  561.2 131.1 %all-gather.14.cloned.1.call-done = bf16[3584,1024]{1,0:T(8,128)(2,1)} async-done(((bf16[896,1024]{1,0:T(8,128)(2,1)}), bf16[3584,1024]{1,0:T(8,128)(2,1)}) %all-gather.14.cloned.1.call-update) | async-done | bytes 7340048 | tf_op jit(solution)/shard_map/all_gather | solution.py:27
  692.3 100.6 %all-gather.12.cloned.1.call-done = bf16[512,3584]{1,0:T(8,128)(2,1)} async-done(((bf16[64,3584]{1,0:T(8,128)(2,1)}), bf16[512,3584]{1,0:T(8,128)(2,1)}) %all-gather.12.cloned.1.call-update) | async-done | bytes 3670032 | tf_op jit(solution)/shard_map/all_gather | solution.py:24
  792.9 9.1 %convolution_convert_fusion.2 = bf16[512,1024]{1,0:T(8,128)(2,1)} fusion(bf16[512,3584]{1,0:T(8,128)(2,1)} %all-gather.12.cloned.1.call-done, bf16[3584,1024]{1,0:T(8,128)(2,1)} %all-gather.14.cloned.1.call-done), kind=kOutput, calls=%fused_computation.2 | convolution fusion | flops 3758620672 | bytes 12058624 | tf_op jit(solution)/shard_map/dot_general | solution.py:25
  802.0 0.0 reduce-scatter.8.cloned.1.call-update
  802.0 30.5 %reduce-scatter.8.cloned.1.call-done = bf16[64,1024]{1,0:T(8,128)(2,1)} async-done(((bf16[512,1024]{1,0:T(8,128)(2,1)}), bf16[64,1024]{1,0:T(8,128)(2,1)}) %reduce-scatter.8.cloned.1.call-update) | async-done | bytes 131088 | tf_op jit(solution)/shard_map/reduce_scatter | solution.py:30
Async XLA Ops:
  6.5 31.6 %all-gather.6.cloned.1.call-start = ((), (), s32[]{:S(2)}) async-start(), calls=%async_computation.3 | async-start | bytes 1179648 | tf_op jit(solution)/shard_map/all_gather | solution.py:8
  7.3 168.4 %all-gather.8.cloned.1.call-start = ((), (), s32[]{:S(2)}) async-start(), calls=%async_computation.4 | async-start | bytes 9175040 | tf_op jit(solution)/shard_map/all_gather | solution.py:13
  8.0 305.1 %all-gather.10.cloned.1.call-start = ((), (), s32[]{:S(2)}) async-start(), calls=%async_computation.6 | async-start | bytes 9175040 | tf_op jit(solution)/shard_map/all_gather | solution.py:14
  8.7 428.9 %reduce-scatter.4.cloned.1.call-start = ((), (), s32[]{:S(2)}) async-start(), calls=%async_computation.5 | async-start | bytes 4128768 | tf_op jit(solution)/shard_map/reduce_scatter | solution.py:16
  38.1 275.0 %copy-start = (bf16[512,1024]{1,0:T(8,128)(2,1)S(1)}, bf16[512,1024]{1,0:T(8,128)(2,1)}, u32[]{:S(2)}) copy-start(bf16[512,1024]{1,0:T(8,128)(2,1)} %all-gather.6.cloned.1.call-done) | copy-start | bytes 3145732
  184.9 374.0 %reduce-scatter.6.cloned.1.call-start = ((), (), s32[]{:S(2)}) async-start(), calls=%async_computation.7 | async-start | bytes 4128768 | tf_op jit(solution)/shard_map/reduce_scatter | solution.py:19
  321.6 370.7 %all-gather.14.cloned.1.call-start = ((), (), s32[]{:S(2)}) async-start(), calls=%async_computation.9 | async-start | bytes 9175040 | tf_op jit(solution)/shard_map/all_gather | solution.py:27
  322.1 470.7 %all-gather.12.cloned.1.call-start = ((), (), s32[]{:S(2)}) async-start(), calls=%async_computation.8 | async-start | bytes 4128768 | tf_op jit(solution)/shard_map/all_gather | solution.py:24
  561.1 271.4 %reduce-scatter.8.cloned.1.call-start = ((), (), s32[]{:S(2)}) async-start(), calls=%async_computation.10 | async-start | bytes 1179648 | tf_op jit(solution)/shard_map/reduce_scatter | solution.py:30
Sparse Core Ops, SparseCore 0:
  9.2 28.8 all-gather.5
  40.0 135.6 all-gather.7
  177.5 135.5 all-gather.9
  317.2 120.3 reduce-scatter.3
  442.3 116.5 reduce-scatter.5
  560.6 131.6 all-gather.13
  694.9 97.9 all-gather.11
  802.1 30.3 reduce-scatter.7
where the time goes:
time: 839 us
  waiting for transfers between devices  797 us (95%)
  matrix products  26.8 us (3%)
  between operations  13.5 us (2%)
    all_gather x1, waiting for transfers between devices, shards(): lax.all_gather(gate_weight, 'gy', axis=1, tiled=True)  138 us
    all_gather x1, waiting for transfers between devices, shards(): lax.all_gather(down_weight, 'gy', axis=0, tiled=True)  131 us
    all_gather x1, waiting for transfers between devices, shards(): lax.all_gather(up_weight, 'gy', axis=1, tiled=True)  128 us
    reduce_scatter x1, waiting for transfers between devices, shards(): lax.psum_scatter(up_partial.astype(jnp.bfloat16), 'gz', scatter_dimension...  121 us
    reduce_scatter x1, waiting for transfers between devices, shards(): lax.psum_scatter(gate_partial.astype(jnp.bfloat16), 'gz', scatter_dimensi...  115 us
    all_gather x1, waiting for transfers between devices, shards(): hidden = lax.all_gather(local_hidden, 'gz', axis=0, tiled=True)  101 us
    reduce_scatter x1, waiting for transfers between devices, shards(): lax.psum_scatter(down_partial.astype(jnp.bfloat16), 'gx', scatter_dimensi...  30.5 us
    all_gather x1, waiting for transfers between devices, shards(): gathered = lax.all_gather(tokens, 'gx', axis=0, tiled=True)  29.3 us
  transfers between devices with their start and end apart: 8, of which 8 were waited for; matrix products, arithmetic and copies ran while one was open for 2% of the time, Pallas kernels for 0%

commit v1 on v0

--- a/solution.py
+++ b/solution.py
@@ -5,7 +5,21 @@
 
 
 def shards(tokens, gate_weight, up_weight, down_weight):
-    gathered = lax.all_gather(tokens, "gx", axis=0, tiled=True)
+    ways, here, lap = (lax.axis_size("gx"), lax.axis_index("gx"), tokens.shape[0])
+    shape = [n * ways if d == 0 else n for d, n in enumerate(tokens.shape)]
+    full = lax.dynamic_update_slice_in_dim(
+        jnp.zeros(shape, tokens.dtype), tokens, here * lap, axis=0
+    )
+    going_up = going_down = tokens
+    for far in range(1, ways // 2 + 1):
+        going_up = lax.ppermute(going_up, "gx", [(d, (d + 1) % ways) for d in range(ways)])
+        full = lax.dynamic_update_slice_in_dim(full, going_up, (here - far) % ways * lap, axis=0)
+        if 2 * far < ways:
+            going_down = lax.ppermute(going_down, "gx", [(d, (d - 1) % ways) for d in range(ways)])
+            full = lax.dynamic_update_slice_in_dim(
+                full, going_down, (here + far) % ways * lap, axis=0
+            )
+    gathered = full
 
     def column_product(weight_piece):
         return jnp.dot(gathered, weight_piece, preferred_element_type=jnp.float32)

time: 839 us -> 810 us (0.965)
  waiting for transfers between devices: 797 us -> 758 us
  starting transfers between devices: 0.28 us -> 9.12 us
    all_gather x1 -> x0, waiting for transfers between devices: 29.3 us -> none  [shards(): gathered = lax.all_gather(tokens, 'gx', axis=0, tiled=True)]
    all_gather x1, waiting for transfers between devices: 138 us -> 117 us  [shards(): lax.all_gather(gate_weight, 'gy', axis=1, tiled=True)]
    ppermute x0 -> x7, waiting for transfers between devices: none -> 12.6 us  [the longest x4 12.6 us: shards(): lax.ppermute(going_up, 'gx', [(d, (d + 1) % ways) for d in range(ways)])]
    ppermute x0 -> x7, starting transfers between devices: none -> 8.88 us  [the longest x3 8.85 us: shards(): lax.ppermute(going_down, 'gx', [(d, (d - 1) % ways) for d in range(ways)])]
  transfers between devices with their start and end apart: 8 -> 14, of which waited for: 8 -> 11; matrix products, arithmetic and copies ran while one was open for 2% -> 3% of each run, Pallas kernels for 0% -> 0%
where the time goes in v1:
time: 810 us
  waiting for transfers between devices  758 us (94%)
  matrix products  26 us (3%)
  between operations  13.6 us (2%)
  starting transfers between devices  9.12 us (1%)
    all_gather x1, waiting for transfers between devices, shards(): lax.all_gather(down_weight, 'gy', axis=0, tiled=True)  131 us
    all_gather x1, waiting for transfers between devices, shards(): lax.all_gather(up_weight, 'gy', axis=1, tiled=True)  129 us
    reduce_scatter x1, waiting for transfers between devices, shards(): lax.psum_scatter(up_partial.astype(jnp.bfloat16), 'gz', scatter_dimension...  119 us
    all_gather x1, waiting for transfers between devices, shards(): lax.all_gather(gate_weight, 'gy', axis=1, tiled=True)  117 us
    reduce_scatter x1, waiting for transfers between devices, shards(): lax.psum_scatter(gate_partial.astype(jnp.bfloat16), 'gz', scatter_dimensi...  116 us
    all_gather x1, waiting for transfers between devices, shards(): hidden = lax.all_gather(local_hidden, 'gz', axis=0, tiled=True)  100 us
    reduce_scatter x1, waiting for transfers between devices, shards(): lax.psum_scatter(down_partial.astype(jnp.bfloat16), 'gx', scatter_dimensi...  30.5 us
    dot_general x2, matrix products, column_product(): return jnp.dot(gathered, weight_piece, preferred_element_type=jnp.float32)  16.9 us
  transfers between devices with their start and end apart: 14, of which 11 were waited for; matrix products, arithmetic and copies ran while one was open for 3% of the time, Pallas kernels for 0%

profile of v1, /device:TPU:2, one launch (start us, length us, event | category | flops | bytes accessed | tf_op | source)
XLA Modules:
  0.0 809.7 jit_solution(5254276412785545997)
XLA Ops:
  6.5 0.7 all-gather.5.cloned.1.call-update
  7.3 0.0 all-gather.7.cloned.1.call-start
  7.3 0.7 all-gather.7.cloned.1.call-update
  8.0 0.0 reduce-scatter.4.cloned.1.call-start
  8.1 0.0 collective-permute-start
  8.1 2.9 collective-permute-start.1
  11.0 0.1 broadcast_in_dim.3
  11.1 0.9 constant_dynamic-update-slice_fusion.7
  12.1 1.8 collective-permute-done
  13.9 3.0 collective-permute-start.3
  16.9 2.6 collective-permute-done.2
  19.5 3.0 collective-permute-start.5
  22.5 2.6 collective-permute-done.4
  25.1 5.5 collective-permute-done.6
  30.7 117.3 %all-gather.5.cloned.1.call-done = bf16[1024,3584]{1,0:T(8,128)(2,1)} async-done(((bf16[1024,896]{1,0:T(8,128)(2,1)}), bf16[1024,3584]{1,0:T(8,128)(2,1)}) %all-gather.5.cloned.1.call-update) | async-done | bytes 7340048 | tf_op jit(solution)/shard_map/all_gather | solution.py:27
  148.0 8.5 %convolution_convert_fusion.1 = bf16[512,3584]{1,0:T(8,128)(2,1)} fusion(bf16[512,1024]{1,0:T(8,128)(2,1)S(1)} %constant_dynamic-update-slice_fusion, bf16[1024,3584]{1,0:T(8,128)(2,1)} %all-gather.5.cloned.1.call-done), kind=kOutput, calls=%fused_computation.1 | convolution fusion | flops 3759931392 | bytes 12058624 | tf_op jit(solution)/shard_map/dot_general | solution.py:25
  156.5 0.0 reduce-scatter.4.cloned.1.call-update
  156.5 0.0 reduce-scatter.6.cloned.1.call-start
  156.6 128.8 %all-gather.7.cloned.1.call-done = bf16[1024,3584]{1,0:T(8,128)(2,1)} async-done(((bf16[1024,896]{1,0:T(8,128)(2,1)}), bf16[1024,3584]{1,0:T(8,128)(2,1)}) %all-gather.7.cloned.1.call-update) | async-done | bytes 7340048 | tf_op jit(solution)/shard_map/all_gather | solution.py:28
  285.4 8.4 %convolution_convert_fusion = bf16[512,3584]{1,0:T(8,128)(2,1)} fusion(bf16[512,1024]{1,0:T(8,128)(2,1)S(1)} %constant_dynamic-update-slice_fusion, bf16[1024,3584]{1,0:T(8,128)(2,1)} %all-gather.7.cloned.1.call-done), kind=kOutput, calls=%fused_computation | convolution fusion | flops 3759931392 | bytes 12058624 | tf_op jit(solution)/shard_map/dot_general | solution.py:25
  293.8 0.0 reduce-scatter.6.cloned.1.call-update
  293.8 0.0 all-gather.11.cloned.1.call-start
  293.9 0.5 all-gather.11.cloned.1.call-update
  294.4 0.0 all-gather.9.cloned.1.call-start
  294.5 115.6 %reduce-scatter.4.cloned.1.call-done = bf16[64,3584]{1,0:T(8,128)(2,1)} async-done(((bf16[512,3584]{1,0:T(8,128)(2,1)}), bf16[64,3584]{1,0:T(8,128)(2,1)}) %reduce-scatter.4.cloned.1.call-update) | async-done | bytes 458768 | tf_op jit(solution)/shard_map/reduce_scatter | solution.py:30
  410.1 119.4 %reduce-scatter.6.cloned.1.call-done = bf16[64,3584]{1,0:T(8,128)(2,1)} async-done(((bf16[512,3584]{1,0:T(8,128)(2,1)}), bf16[64,3584]{1,0:T(8,128)(2,1)}) %reduce-scatter.6.cloned.1.call-update) | async-done | bytes 458768 | tf_op jit(solution)/shard_map/reduce_scatter | solution.py:33
  529.5 2.2 fusion.4
  531.7 0.0 reduce-scatter.8.cloned.1.call-start
  531.8 131.0 %all-gather.11.cloned.1.call-done = bf16[3584,1024]{1,0:T(8,128)(2,1)} async-done(((bf16[896,1024]{1,0:T(8,128)(2,1)}), bf16[3584,1024]{1,0:T(8,128)(2,1)}) %all-gather.11.cloned.1.call-update) | async-done | bytes 7340048 | tf_op jit(solution)/shard_map/all_gather | solution.py:41
  662.8 100.5 %all-gather.9.cloned.1.call-done = bf16[512,3584]{1,0:T(8,128)(2,1)} async-done(((bf16[64,3584]{1,0:T(8,128)(2,1)}), bf16[512,3584]{1,0:T(8,128)(2,1)}) %all-gather.9.cloned.1.call-update) | async-done | bytes 3670032 | tf_op jit(solution)/shard_map/all_gather | solution.py:38
  763.3 9.1 %convolution_convert_fusion.2 = bf16[512,1024]{1,0:T(8,128)(2,1)} fusion(bf16[512,3584]{1,0:T(8,128)(2,1)} %all-gather.9.cloned.1.call-done, bf16[3584,1024]{1,0:T(8,128)(2,1)} %all-gather.11.cloned.1.call-done), kind=kOutput, calls=%fused_computation.2 | convolution fusion | flops 3758620672 | bytes 12058624 | tf_op jit(solution)/shard_map/dot_general | solution.py:39
  772.4 30.5 %reduce-scatter.8.cloned.1.call-done = bf16[64,1024]{1,0:T(8,128)(2,1)} async-done(((bf16[512,1024]{1,0:T(8,128)(2,1)}), bf16[64,1024]{1,0:T(8,128)(2,1)}) %reduce-scatter.8.cloned.1.call-update) | async-done | bytes 131088 | tf_op jit(solution)/shard_map/reduce_scatter | solution.py:44
  (16 shorter events, 0.1 us)
Async XLA Ops:
  6.5 141.5 %all-gather.5.cloned.1.call-start = ((), (), s32[]{:S(2)}) async-start(), calls=%async_computation.3 | async-start | bytes 9175040 | tf_op jit(solution)/shard_map/all_gather | solution.py:27
  7.3 278.1 %all-gather.7.cloned.1.call-start = ((), (), s32[]{:S(2)}) async-start(), calls=%async_computation.5 | async-start | bytes 9175040 | tf_op jit(solution)/shard_map/all_gather | solution.py:28
  8.0 402.1 %reduce-scatter.4.cloned.1.call-start = ((), (), s32[]{:S(2)}) async-start(), calls=%async_computation.4 | async-start | bytes 4128768 | tf_op jit(solution)/shard_map/reduce_scatter | solution.py:30
  8.1 5.8 collective-permute-start
  8.1 5.8 collective-permute-start.1
  13.9 5.6 collective-permute-start.2
  13.9 5.6 collective-permute-start.3
  19.5 5.6 collective-permute-start.4
  19.5 5.6 collective-permute-start.5
  25.1 5.6 collective-permute-start.6
  156.5 373.0 %reduce-scatter.6.cloned.1.call-start = ((), (), s32[]{:S(2)}) async-start(), calls=%async_computation.6 | async-start | bytes 4128768 | tf_op jit(solution)/shard_map/reduce_scatter | solution.py:33
  293.8 369.0 %all-gather.11.cloned.1.call-start = ((), (), s32[]{:S(2)}) async-start(), calls=%async_computation.8 | async-start | bytes 9175040 | tf_op jit(solution)/shard_map/all_gather | solution.py:41
  294.4 468.8 %all-gather.9.cloned.1.call-start = ((), (), s32[]{:S(2)}) async-start(), calls=%async_computation.7 | async-start | bytes 4128768 | tf_op jit(solution)/shard_map/all_gather | solution.py:38
  531.7 271.2 %reduce-scatter.8.cloned.1.call-start = ((), (), s32[]{:S(2)}) async-start(), calls=%async_computation.9 | async-start | bytes 1179648 | tf_op jit(solution)/shard_map/reduce_scatter | solution.py:44
Sparse Core Ops, SparseCore 0:
  9.2 138.7 all-gather.4
  149.8 135.5 all-gather.6
  289.6 120.4 reduce-scatter.3
  414.8 114.6 reduce-scatter.5
  531.1 131.6 all-gather.10
  665.3 97.9 all-gather.8
  772.5 30.3 reduce-scatter.7
